TPU v7x, 32 devices: a whole 2x2x4 slice. The times are simulated.
32 devices in a mesh: pairs: 2 (over y), blk: 8 (over z, x), panel: 2 (over core).
Axes of the slice: x: 2, y: 2, z: 4, core: 2. Of those that a mesh axis runs over, the one named last changes fastest.
Arguments:
- first_frame: bfloat16 [4096, 256], P(('pairs', 'blk', 'panel')), parts along dimension 0, may hold values from -8 to 8
- second_frame: bfloat16 [16, 8, 16, 256], P(('pairs', 'blk'), None, 'panel'), parts along dimension 0, may hold values from -8 to 8
Outputs:
- matched: float32 [4, 2, 4096], P(None, None, ('pairs', 'blk', 'panel')), parts along dimension 2
- energy: float32 [4, 4096], P(None, ('pairs', 'blk', 'panel')), parts along dimension 1
There are 2 independent parts, one for each index of `pairs`. A program takes and returns all parts, laid end to end along the dimension named above; each array names one. Nothing has to cross between parts.
All inputs are finite; a program needn't handle non-finite values.
Results may differ from a plain program's by a relative error of at most 0.014.
Values may be sent and summed in bfloat16 or wider, within the bound.
A program may use at most 128 MiB of HBM per device.

v0:
```python
import math
import jax
import jax.numpy as jnp
from jax import lax
from jax.sharding import PartitionSpec as P

LEVELS = 4
COLBLK = 8
BCOLS = 16
neg_large = -1e30


def build_levels(tile_batch):
    result = [tile_batch]
    pooled = tile_batch.astype(jnp.float32)
    for level_index in range(1, LEVELS):
        tile_count, height, columns, channels = pooled.shape
        pooled = pooled.reshape(tile_count, height // 2, 2, columns // 2, 2, channels).mean(
            axis=(2, 4)
        )
        result.append(pooled.astype(jnp.bfloat16))
    return result


def accumulate(carry_state, level_pieces, queries, col_start, total_rows, total_cols):
    maxima, totals = carry_state
    new_maxima = []
    new_totals = []
    for level_index in range(len(level_pieces)):
        level_piece = level_pieces[level_index]
        tile_count, height, columns, channels = level_piece.shape
        key_rows = level_piece.reshape(tile_count * height * columns, channels)
        factor = 3.0 * 2.0**level_index / math.sqrt(channels)
        scores = (
            jnp.einsum("kc,qc->kq", key_rows, queries, preferred_element_type=jnp.float32) * factor
        )
        merged_top = jnp.maximum(maxima[level_index], jnp.max(scores, axis=0))
        weights = jnp.exp(scores - merged_top[None, :])
        spacing = 2**level_index
        block_ids = jnp.arange(tile_count)
        row_index = (block_ids // COLBLK)[:, None, None] * height + jnp.arange(height)[
            None, :, None
        ]
        col_index = (
            (block_ids % COLBLK)[:, None, None] * (BCOLS // spacing)
            + col_start // spacing
            + jnp.arange(columns)[None, None, :]
        )
        row_grid = jnp.broadcast_to(row_index, (tile_count, height, columns)).astype(jnp.float32)
        col_grid = jnp.broadcast_to(col_index, (tile_count, height, columns)).astype(jnp.float32)
        row_pos = (row_grid + 0.5) * (float(spacing) / total_rows)
        col_pos = (col_grid + 0.5) * (float(spacing) / total_cols)
        unit_row = jnp.ones_like(row_pos)
        position_rows = jnp.stack([unit_row.reshape(-1), row_pos.reshape(-1), col_pos.reshape(-1)])
        block_totals = jnp.dot(
            position_rows,
            weights,
            precision=lax.Precision.HIGHEST,
            preferred_element_type=jnp.float32,
        )
        rescale = jnp.exp(maxima[level_index] - merged_top)
        new_totals.append(totals[level_index] * rescale[None, :] + block_totals)
        new_maxima.append(merged_top)
    return (jnp.stack(new_maxima), jnp.stack(new_totals))


def body(first_frame, second_frame):
    cycle_size = lax.axis_size("blk")
    panels = lax.axis_size("panel")
    block_count, tile_rows, tile_cols, channels = second_frame.shape
    total_rows = tile_rows * cycle_size // COLBLK
    total_cols = BCOLS * COLBLK
    col_start = lax.axis_index("panel") * tile_cols
    queries = lax.all_gather(first_frame, "panel", axis=0, tiled=True)
    query_count = queries.shape[0]
    init_state = (
        jnp.full((LEVELS, query_count), neg_large, jnp.float32),
        jnp.zeros((LEVELS, 3, query_count), jnp.float32),
    )
    level_zero, level_one, level_two, level_three = build_levels(second_frame)
    maxima, totals = accumulate(
        init_state,
        list(
            (
                lax.all_gather(level_zero, "blk", axis=0, tiled=True),
                lax.all_gather(level_one, "blk", axis=0, tiled=True),
                lax.all_gather(level_two, "blk", axis=0, tiled=True),
                lax.all_gather(level_three, "blk", axis=0, tiled=True),
            )
        ),
        queries,
        col_start,
        total_rows,
        total_cols,
    )
    half_count = query_count // panels
    own_max, own_tot = (
        lax.all_to_all(
            maxima.reshape(LEVELS, 1, panels, half_count),
            "panel",
            split_axis=2,
            concat_axis=2,
            tiled=True,
        ),
        lax.all_to_all(
            totals.reshape(LEVELS, 3, panels, half_count),
            "panel",
            split_axis=2,
            concat_axis=2,
            tiled=True,
        ),
    )
    merged = jnp.max(own_max, axis=2)
    totals = jnp.sum(own_tot * jnp.exp(own_max - merged[:, :, None, :]), axis=2)
    maxima = merged[:, 0, :]
    energy = maxima + jnp.log(totals[:, 0, :])
    matched = totals[:, 1:, :] / totals[:, 0:1, :]
    return (matched, energy)


def solution(mesh):
    placed = (P(("pairs", "blk", "panel"), None), P(("pairs", "blk"), None, "panel", None))
    return jax.shard_map(
        body,
        mesh=mesh,
        in_specs=placed,
        out_specs=(P(None, None, ("pairs", "blk", "panel")), P(None, ("pairs", "blk", "panel"))),
        check_vma=False,
    )
```

profile of v0, /device:TPU:0, one launch (start us, length us, event | category | flops | bytes accessed | tf_op | source)
XLA Modules:
  0.0 125.8 jit_solution(9972526232094171274)
XLA Ops:
  0.6 0.9 reshape.573
  1.5 32.7 %all_gather.15 = bf16[8,8,8,256]{3,2,1,0:T(8,128)(2,1)S(1)} all-gather(bf16[1,8,8,256]{3,2,1,0:T(8,128)(2,1)S(1)} %copy-done), channel_id=1, replica_groups=mesh['pairs'=2,'blk'=8,'panel'=2] {'blk'}, dimensions={0}, use_global_device_ids=true | all-gather | bytes 294912 | tf_op jit(solution)/shard_map/all_gather | solution.py:85
  34.2 1.9 %all_gather.16 = bf16[256,256]{1,0:T(8,128)(2,1)S(1)} all-gather(bf16[128,256]{1,0:T(8,128)(2,1)S(1)} %copy-done.1), channel_id=1, replica_groups=mesh['pairs'=2,'blk'=8,'panel'=2] {'panel'}, dimensions={0}, use_global_device_ids=true | all-gather | bytes 196608 | tf_op jit(solution)/shard_map/all_gather | solution.py:74
  36.2 30.5 %all-gather = bf16[32,4,256]{2,1,0:T(4,128)(2,1)S(1)} all-gather(bf16[4,4,256]{2,1,0:T(4,128)(2,1)S(1)} %get-tuple-element.6), channel_id=2, replica_groups=mesh['pairs'=2,'blk'=8,'panel'=2] {'blk'}, dimensions={0}, use_global_device_ids=true | all-gather | bytes 73728 | tf_op jit(solution)/shard_map/all_gather | solution.py:86
  66.7 0.2 fusion.48
  67.0 26.1 %all-gather.1 = bf16[16,2,256]{2,1,0:T(2,128)(2,1)S(1)} all-gather(bf16[2,2,256]{2,1,0:T(2,128)(2,1)S(1)} %get-tuple-element.8), channel_id=3, replica_groups=mesh['pairs'=2,'blk'=8,'panel'=2] {'blk'}, dimensions={0}, use_global_device_ids=true | all-gather | bytes 18432 | tf_op jit(solution)/shard_map/all_gather | solution.py:87
  93.2 0.2 fusion.47
  93.4 19.0 %all-gather.3 = bf16[8,1,256]{2,1,0:T(2,128)(2,1)S(1)} all-gather(bf16[1,1,256]{2,1,0:T(2,128)(2,1)S(1)} %reshape.580), channel_id=4, replica_groups=mesh['pairs'=2,'blk'=8,'panel'=2] {'blk'}, dimensions={0}, use_global_device_ids=true | all-gather | bytes 4608 | tf_op jit(solution)/shard_map/all_gather | solution.py:88
  112.4 0.2 fusion.46
  112.7 0.3 fusion.49
  113.0 0.6 pad_maximum_fusion.1
  113.6 3.2 %all-to-all-start.1 = ((f32[4,1,2,128]{3,0,1,2:T(4,128)}), f32[4,1,2,128]{3,0,1,2:T(4,128)S(1)}, u32[]{:S(2)}, u32[]{:S(2)}) async-start(f32[4,1,2,128]{3,0,1,2:T(4,128)} %pad_maximum_fusion.1), calls=%async_computation.1 | async-start | bytes 8192 | tf_op jit(solution)/shard_map/all_to_all | solution.py:98
  117.0 0.1 mul.250
  117.2 0.1 mul.246
  117.4 0.2 convolution_add_fusion.2
  118.0 0.1 mul.256
  118.1 0.2 convolution_add_fusion.1
  118.3 0.2 convolution_add_fusion
  119.0 0.3 convolution_add_fusion.3
  119.4 0.6 pad_maximum_fusion
  120.0 3.2 %all-to-all-start = ((f32[4,3,2,128]{3,0,1,2:T(4,128)}), f32[4,3,2,128]{3,0,1,2:T(4,128)S(1)}, u32[]{:S(2)}, u32[]{:S(2)}) async-start(f32[4,3,2,128]{3,0,1,2:T(4,128)} %pad_maximum_fusion), calls=%async_computation | async-start | bytes 24576 | tf_op jit(solution)/shard_map/all_to_all | solution.py:105
  123.3 1.3 %all-to-all-done = f32[4,3,2,128]{3,0,1,2:T(4,128)S(1)} async-done(((f32[4,3,2,128]{3,0,1,2:T(4,128)}), f32[4,3,2,128]{3,0,1,2:T(4,128)S(1)}, u32[]{:S(2)}, u32[]{:S(2)}) %all-to-all-start) | async-done | bytes 12320 | tf_op jit(solution)/shard_map/all_to_all | solution.py:105
  124.6 0.6 log_add_fusion
  125.2 0.6 copy_divide_fusion
  (54 shorter events, 1.4 us)
Async XLA Ops:
  0.6 0.9 copy-start
  1.5 32.7 %copy-start.1 = (bf16[128,256]{1,0:T(8,128)(2,1)S(1)}, bf16[128,256]{1,0:T(8,128)(2,1)}, u32[]{:S(2)}) copy-start(bf16[128,256]{1,0:T(8,128)(2,1)} %param.2) | copy-start | bytes 196612
  113.6 6.4 %all-to-all-start.1 = ((f32[4,1,2,128]{3,0,1,2:T(4,128)}), f32[4,1,2,128]{3,0,1,2:T(4,128)S(1)}, u32[]{:S(2)}, u32[]{:S(2)}) async-start(f32[4,1,2,128]{3,0,1,2:T(4,128)} %pad_maximum_fusion.1), calls=%async_computation.1 | async-start | bytes 8192 | tf_op jit(solution)/shard_map/all_to_all | solution.py:98
  120.0 4.6 %all-to-all-start = ((f32[4,3,2,128]{3,0,1,2:T(4,128)}), f32[4,3,2,128]{3,0,1,2:T(4,128)S(1)}, u32[]{:S(2)}, u32[]{:S(2)}) async-start(f32[4,3,2,128]{3,0,1,2:T(4,128)} %pad_maximum_fusion), calls=%async_computation | async-start | bytes 24576 | tf_op jit(solution)/shard_map/all_to_all | solution.py:105
where the time goes:
time: 126 us
  blocking collectives  110 us (87%)
  starting transfers between devices  6.45 us (5%)
  other arithmetic  3.09 us (2%)
  local copies, waits for them, and re-layouts  1.92 us (2%)
  matrix products  1.83 us (1%)
  waiting for transfers between devices  1.33 us (1%)
    all_gather x1, blocking collectives, body(): lax.all_gather(level_zero, 'blk', axis=0, tiled=True)  32.7 us
    all_gather x1, blocking collectives, body(): lax.all_gather(level_one, 'blk', axis=0, tiled=True)  30.5 us
    all_gather x1, blocking collectives, body(): lax.all_gather(level_two, 'blk', axis=0, tiled=True)  26.1 us
    all_gather x1, blocking collectives, body(): lax.all_gather(level_three, 'blk', axis=0, tiled=True)  19 us
    all_to_all x1, starting transfers between devices, body(): lax.all_to_all(totals.reshape(LEVELS, 3, panels, half_count), 'panel', sp...  3.23 us
    all_to_all x1, starting transfers between devices, body(): lax.all_to_all(maxima.reshape(LEVELS, 1, panels, half_count), 'panel', sp...  3.22 us
  transfers between devices with their start and end apart: 2, of which 1 were waited for; matrix products, arithmetic and copies ran while one was open for 2% of the time, Pallas kernels for 0%

commit v1 on v0

--- a/solution.py
+++ b/solution.py
@@ -8,6 +8,19 @@
 COLBLK = 8
 BCOLS = 16
 neg_large = -1e30
+
+
+def collect(shard, axis, dim):
+    ways = lax.axis_size(axis)
+    up = [(d, (d + 1) % ways) for d in range(ways)]
+    down = [(d, (d - 1) % ways) for d in range(ways)]
+    earlier, later = ([shard], [shard])
+    for _ in range(ways // 2):
+        earlier.append(lax.ppermute(earlier[-1], axis, up))
+    for _ in range((ways - 1) // 2):
+        later.append(lax.ppermute(later[-1], axis, down))
+    line = jnp.concatenate([*earlier[::-1], *later[1:]], axis=dim)
+    return jnp.roll(line, (lax.axis_index(axis) - ways // 2) * shard.shape[dim], axis=dim)
 
 
 def build_levels(tile_batch):
@@ -83,7 +96,7 @@
         list(
             (
                 lax.all_gather(level_zero, "blk", axis=0, tiled=True),
-                lax.all_gather(level_one, "blk", axis=0, tiled=True),
+                collect(level_one, "blk", 0),
                 lax.all_gather(level_two, "blk", axis=0, tiled=True),
                 lax.all_gather(level_three, "blk", axis=0, tiled=True),
             )

time: 126 us -> 119 us (0.944)
  blocking collectives: 110 us -> 77.1 us
  starting transfers between devices: 6.45 us -> 22.1 us
  waiting for transfers between devices: 1.33 us -> 11.2 us
    all_gather x1 -> x0, blocking collectives: 30.5 us -> none  [body(): lax.all_gather(level_one, 'blk', axis=0, tiled=True)]
    ppermute x0 -> x7, starting transfers between devices: none -> 15.7 us  [the longest x3 12.6 us: collect(): later.append(lax.ppermute(later[-1], axis, down))]
    ppermute x0 -> x7, waiting for transfers between devices: none -> 9.15 us  [the longest x4 8.97 us: collect(): earlier.append(lax.ppermute(earlier[-1], axis, up))]
    all_gather x1, blocking collectives: 32.7 us -> 30.9 us  [body(): lax.all_gather(level_zero, 'blk', axis=0, tiled=True)]
  transfers between devices with their start and end apart: 2 -> 9, of which waited for: 1 -> 6; matrix products, arithmetic and copies ran while one was open for 2% -> 3% of each run, Pallas kernels for 0% -> 0%
where the time goes in v1:
time: 119 us; the launch traced here: 118 us
  blocking collectives  77.1 us (65%)
  starting transfers between devices  22.1 us (19%)
  waiting for transfers between devices  11.2 us (9%)
  other arithmetic  3.13 us (3%)
  local copies, waits for them, and re-layouts  2.03 us (2%)
  matrix products  1.85 us (2%)
    all_gather x1, blocking collectives, body(): lax.all_gather(level_zero, 'blk', axis=0, tiled=True)  30.9 us
    all_gather x1, blocking collectives, body(): lax.all_gather(level_two, 'blk', axis=0, tiled=True)  26.1 us
    all_gather x1, blocking collectives, body(): lax.all_gather(level_three, 'blk', axis=0, tiled=True)  18.2 us
    ppermute x3, starting transfers between devices, collect(): later.append(lax.ppermute(later[-1], axis, down))  12.6 us
    ppermute x4, waiting for transfers between devices, collect(): earlier.append(lax.ppermute(earlier[-1], axis, up))  8.97 us
    all_to_all x1, starting transfers between devices, body(): lax.all_to_all(totals.reshape(LEVELS, 3, panels, half_count), 'panel', sp...  3.23 us
    all_to_all x1, starting transfers between devices, body(): lax.all_to_all(maxima.reshape(LEVELS, 1, panels, half_count), 'panel', sp...  3.22 us
    ppermute x4, starting transfers between devices, collect(): earlier.append(lax.ppermute(earlier[-1], axis, up))  3.08 us
  transfers between devices with their start and end apart: 9, of which 6 were waited for; matrix products, arithmetic and copies ran while one was open for 3% of the time, Pallas kernels for 0%

profile of v1, /device:TPU:0, one launch (start us, length us, event | category | flops | bytes accessed | tf_op | source)
XLA Modules:
  0.0 118.5 jit_solution(9881526643543207897)
XLA Ops:
  0.6 0.8 reshape.573
  1.5 3.0 %collective-permute-start = (bf16[1,4,4,256]{3,2,1,0:T(4,128)(2,1)S(1)}, bf16[1,4,4,256]{3,2,1,0:T(4,128)(2,1)S(1)}, u32[]{:S(2)}, u32[]{:S(2)}) collective-permute-start(bf16[1,4,4,256]{3,2,1,0:T(4,128)(2,1)S(1)} %get-tuple-element.6), channel_id=1, source_target_pairs={{0,2},{2,4},{4,6},{6,8},{8,10},{10,12},{12,14},{14,0},{1,3},{3,5},... | collective-permute-start | bytes 24584 | tf_op jit(solution)/shard_map/ppermute | solution.py:19
  4.5 3.1 %collective-permute-start.4 = (bf16[1,4,4,256]{3,2,1,0:T(4,128)(2,1)S(1)}, bf16[1,4,4,256]{3,2,1,0:T(4,128)(2,1)S(1)}, u32[]{:S(2)}, u32[]{:S(2)}) collective-permute-start(bf16[1,4,4,256]{3,2,1,0:T(4,128)(2,1)S(1)} %get-tuple-element.6), channel_id=1, source_target_pairs={{0,14},{2,0},{4,2},{6,4},{8,6},{10,8},{12,10},{14,12},{1,15},{3,1}... | collective-permute-start | bytes 24584 | tf_op jit(solution)/shard_map/ppermute | solution.py:21
  7.6 30.9 %all_gather.12 = bf16[8,8,8,256]{3,2,1,0:T(8,128)(2,1)S(1)} all-gather(bf16[1,8,8,256]{3,2,1,0:T(8,128)(2,1)S(1)} %copy-done), channel_id=1, replica_groups=mesh['pairs'=2,'blk'=8,'panel'=2] {'blk'}, dimensions={0}, use_global_device_ids=true | all-gather | bytes 294912 | tf_op jit(solution)/shard_map/all_gather | solution.py:98
  38.6 1.9 %all_gather.13 = bf16[256,256]{1,0:T(8,128)(2,1)S(1)} all-gather(bf16[128,256]{1,0:T(8,128)(2,1)S(1)} %copy-done.1), channel_id=1, replica_groups=mesh['pairs'=2,'blk'=8,'panel'=2] {'panel'}, dimensions={0}, use_global_device_ids=true | all-gather | bytes 196608 | tf_op jit(solution)/shard_map/all_gather | solution.py:87
  40.6 18.2 %all-gather.2 = bf16[8,1,256]{2,1,0:T(2,128)(2,1)S(1)} all-gather(bf16[1,1,256]{2,1,0:T(2,128)(2,1)S(1)} %reshape.578), channel_id=3, replica_groups=mesh['pairs'=2,'blk'=8,'panel'=2] {'blk'}, dimensions={0}, use_global_device_ids=true | all-gather | bytes 4608 | tf_op jit(solution)/shard_map/all_gather | solution.py:101
  59.0 26.1 %all-gather = bf16[16,2,256]{2,1,0:T(2,128)(2,1)S(1)} all-gather(bf16[2,2,256]{2,1,0:T(2,128)(2,1)S(1)} %get-tuple-element.8), channel_id=2, replica_groups=mesh['pairs'=2,'blk'=8,'panel'=2] {'blk'}, dimensions={0}, use_global_device_ids=true | all-gather | bytes 18432 | tf_op jit(solution)/shard_map/all_gather | solution.py:100
  85.8 0.3 fusion.48
  87.0 0.3 convolution_add_fusion.3
  87.5 6.3 %collective-permute-done.1 = bf16[1,4,4,256]{3,2,1,0:T(4,128)(2,1)S(1)} collective-permute-done((bf16[1,4,4,256]{3,2,1,0:T(4,128)(2,1)S(1)}, bf16[1,4,4,256]{3,2,1,0:T(4,128)(2,1)S(1)}, u32[]{:S(2)}, u32[]{:S(2)}) %collective-permute-start.1) | collective-permute-done | bytes 8224 | tf_op jit(solution)/shard_map/ppermute | solution.py:19
  93.8 4.7 %collective-permute-start.5 = (bf16[1,4,4,256]{3,2,1,0:T(4,128)(2,1)S(1)}, bf16[1,4,4,256]{3,2,1,0:T(4,128)(2,1)S(1)}, u32[]{:S(2)}, u32[]{:S(2)}) collective-permute-start(bf16[1,4,4,256]{3,2,1,0:T(4,128)(2,1)S(1)} %collective-permute-done.4), channel_id=1, source_target_pairs={{0,14},{2,0},{4,2},{6,4},{8,6},{10,8},{12,10},{14,12},{1,15},{3,1}... | collective-permute-start | bytes 24584 | tf_op jit(solution)/shard_map/ppermute | solution.py:21
  98.5 1.6 %collective-permute-done.2 = bf16[1,4,4,256]{3,2,1,0:T(4,128)(2,1)S(1)} collective-permute-done((bf16[1,4,4,256]{3,2,1,0:T(4,128)(2,1)S(1)}, bf16[1,4,4,256]{3,2,1,0:T(4,128)(2,1)S(1)}, u32[]{:S(2)}, u32[]{:S(2)}) %collective-permute-start.2) | collective-permute-done | bytes 8224 | tf_op jit(solution)/shard_map/ppermute | solution.py:19
  100.6 4.8 %collective-permute-start.6 = (bf16[1,4,4,256]{3,2,1,0:T(4,128)(2,1)S(1)}, bf16[1,4,4,256]{3,2,1,0:T(4,128)(2,1)S(1)}, u32[]{:S(2)}, u32[]{:S(2)}) collective-permute-start(bf16[1,4,4,256]{3,2,1,0:T(4,128)(2,1)S(1)} %collective-permute-done.5), channel_id=1, source_target_pairs={{0,14},{2,0},{4,2},{6,4},{8,6},{10,8},{12,10},{14,12},{1,15},{3,1}... | collective-permute-start | bytes 24584 | tf_op jit(solution)/shard_map/ppermute | solution.py:21
  105.4 1.1 collective-permute-done.3
  107.0 0.2 fusion.47
  107.2 0.2 convolution_add_fusion.2
  107.4 0.6 pad_maximum_fusion.1
  108.1 3.2 %all-to-all-start.1 = ((f32[4,1,2,128]{3,0,1,2:T(4,128)}), f32[4,1,2,128]{3,0,1,2:T(4,128)S(1)}, u32[]{:S(2)}, u32[]{:S(2)}) async-start(f32[4,1,2,128]{3,0,1,2:T(4,128)} %pad_maximum_fusion.1), calls=%async_computation.1 | async-start | bytes 8192 | tf_op jit(solution)/shard_map/all_to_all | solution.py:111
  111.3 0.6 pad_maximum_fusion
  111.9 0.7 all-to-all-done.1
  112.6 3.2 %all-to-all-start = ((f32[4,3,2,128]{3,0,1,2:T(4,128)}), f32[4,3,2,128]{3,0,1,2:T(4,128)S(1)}, u32[]{:S(2)}, u32[]{:S(2)}) async-start(f32[4,3,2,128]{3,0,1,2:T(4,128)} %pad_maximum_fusion), calls=%async_computation | async-start | bytes 24576 | tf_op jit(solution)/shard_map/all_to_all | solution.py:118
  115.9 1.3 %all-to-all-done = f32[4,3,2,128]{3,0,1,2:T(4,128)S(1)} async-done(((f32[4,3,2,128]{3,0,1,2:T(4,128)}), f32[4,3,2,128]{3,0,1,2:T(4,128)S(1)}, u32[]{:S(2)}, u32[]{:S(2)}) %all-to-all-start) | async-done | bytes 12320 | tf_op jit(solution)/shard_map/all_to_all | solution.py:118
  117.3 0.6 log_add_fusion
  117.9 0.6 copy_divide_fusion
  (84 shorter events, 3.0 us)
Async XLA Ops:
  1.5 6.2 %copy-start = (bf16[1,8,8,256]{3,2,1,0:T(8,128)(2,1)S(1)}, bf16[1,8,8,256]{3,2,1,0:T(8,128)(2,1)}, u32[]{:S(2)}) copy-start(bf16[1,8,8,256]{3,2,1,0:T(8,128)(2,1)} %param.3) | copy-start | bytes 98308
  1.5 85.9 %collective-permute-start = (bf16[1,4,4,256]{3,2,1,0:T(4,128)(2,1)S(1)}, bf16[1,4,4,256]{3,2,1,0:T(4,128)(2,1)S(1)}, u32[]{:S(2)}, u32[]{:S(2)}) collective-permute-start(bf16[1,4,4,256]{3,2,1,0:T(4,128)(2,1)S(1)} %get-tuple-element.6), channel_id=1, source_target_pairs={{0,2},{2,4},{4,6},{6,8},{8,10},{10,12},{12,14},{14,0},{1,3},{3,5},... | collective-permute-start | bytes 24584 | tf_op jit(solution)/shard_map/ppermute | solution.py:19
  4.5 89.3 %collective-permute-start.4 = (bf16[1,4,4,256]{3,2,1,0:T(4,128)(2,1)S(1)}, bf16[1,4,4,256]{3,2,1,0:T(4,128)(2,1)S(1)}, u32[]{:S(2)}, u32[]{:S(2)}) collective-permute-start(bf16[1,4,4,256]{3,2,1,0:T(4,128)(2,1)S(1)} %get-tuple-element.6), channel_id=1, source_target_pairs={{0,14},{2,0},{4,2},{6,4},{8,6},{10,8},{12,10},{14,12},{1,15},{3,1}... | collective-permute-start | bytes 24584 | tf_op jit(solution)/shard_map/ppermute | solution.py:21
  7.6 30.9 %copy-start.1 = (bf16[128,256]{1,0:T(8,128)(2,1)S(1)}, bf16[128,256]{1,0:T(8,128)(2,1)}, u32[]{:S(2)}) copy-start(bf16[128,256]{1,0:T(8,128)(2,1)} %param.2) | copy-start | bytes 196612
  87.4 6.4 %collective-permute-start.1 = (bf16[1,4,4,256]{3,2,1,0:T(4,128)(2,1)S(1)}, bf16[1,4,4,256]{3,2,1,0:T(4,128)(2,1)S(1)}, u32[]{:S(2)}, u32[]{:S(2)}) collective-permute-start(bf16[1,4,4,256]{3,2,1,0:T(4,128)(2,1)S(1)} %collective-permute-done), channel_id=1, source_target_pairs={{0,2},{2,4},{4,6},{6,8},{8,10},{10,12},{12,14},{14,0},{1,3},{3,5},... | collective-permute-start | bytes 24584 | tf_op jit(solution)/shard_map/ppermute | solution.py:19
  93.8 6.3 %collective-permute-start.2 = (bf16[1,4,4,256]{3,2,1,0:T(4,128)(2,1)S(1)}, bf16[1,4,4,256]{3,2,1,0:T(4,128)(2,1)S(1)}, u32[]{:S(2)}, u32[]{:S(2)}) collective-permute-start(bf16[1,4,4,256]{3,2,1,0:T(4,128)(2,1)S(1)} %collective-permute-done.1), channel_id=1, source_target_pairs={{0,2},{2,4},{4,6},{6,8},{8,10},{10,12},{12,14},{14,0},{1,3},{3,5},... | collective-permute-start | bytes 24584 | tf_op jit(solution)/shard_map/ppermute | solution.py:19
  93.8 6.8 %collective-permute-start.5 = (bf16[1,4,4,256]{3,2,1,0:T(4,128)(2,1)S(1)}, bf16[1,4,4,256]{3,2,1,0:T(4,128)(2,1)S(1)}, u32[]{:S(2)}, u32[]{:S(2)}) collective-permute-start(bf16[1,4,4,256]{3,2,1,0:T(4,128)(2,1)S(1)} %collective-permute-done.4), channel_id=1, source_target_pairs={{0,14},{2,0},{4,2},{6,4},{8,6},{10,8},{12,10},{14,12},{1,15},{3,1}... | collective-permute-start | bytes 24584 | tf_op jit(solution)/shard_map/ppermute | solution.py:21
  100.1 6.3 %collective-permute-start.3 = (bf16[1,4,4,256]{3,2,1,0:T(4,128)(2,1)S(1)}, bf16[1,4,4,256]{3,2,1,0:T(4,128)(2,1)S(1)}, u32[]{:S(2)}, u32[]{:S(2)}) collective-permute-start(bf16[1,4,4,256]{3,2,1,0:T(4,128)(2,1)S(1)} %collective-permute-done.2), channel_id=1, source_target_pairs={{0,2},{2,4},{4,6},{6,8},{8,10},{10,12},{12,14},{14,0},{1,3},{3,5},... | collective-permute-start | bytes 24584 | tf_op jit(solution)/shard_map/ppermute | solution.py:19
  100.6 6.1 %collective-permute-start.6 = (bf16[1,4,4,256]{3,2,1,0:T(4,128)(2,1)S(1)}, bf16[1,4,4,256]{3,2,1,0:T(4,128)(2,1)S(1)}, u32[]{:S(2)}, u32[]{:S(2)}) collective-permute-start(bf16[1,4,4,256]{3,2,1,0:T(4,128)(2,1)S(1)} %collective-permute-done.5), channel_id=1, source_target_pairs={{0,14},{2,0},{4,2},{6,4},{8,6},{10,8},{12,10},{14,12},{1,15},{3,1}... | collective-permute-start | bytes 24584 | tf_op jit(solution)/shard_map/ppermute | solution.py:21
  108.1 4.6 %all-to-all-start.1 = ((f32[4,1,2,128]{3,0,1,2:T(4,128)}), f32[4,1,2,128]{3,0,1,2:T(4,128)S(1)}, u32[]{:S(2)}, u32[]{:S(2)}) async-start(f32[4,1,2,128]{3,0,1,2:T(4,128)} %pad_maximum_fusion.1), calls=%async_computation.1 | async-start | bytes 8192 | tf_op jit(solution)/shard_map/all_to_all | solution.py:111
  112.6 4.6 %all-to-all-start = ((f32[4,3,2,128]{3,0,1,2:T(4,128)}), f32[4,3,2,128]{3,0,1,2:T(4,128)S(1)}, u32[]{:S(2)}, u32[]{:S(2)}) async-start(f32[4,3,2,128]{3,0,1,2:T(4,128)} %pad_maximum_fusion), calls=%async_computation | async-start | bytes 24576 | tf_op jit(solution)/shard_map/all_to_all | solution.py:118
